TPU v7x, 32 devices: a whole 2x2x4 slice. The times are simulated.
32 devices in a mesh: energy: 8 (over y, x, core), kpt: 4 (over z).
Axes of the slice: x: 2, y: 2, z: 4, core: 2. Of those that a mesh axis runs over, the one named last changes fastest.
Arguments:
- density: bfloat16 [32, 4, 64, 3072], P('energy', 'kpt'), may hold values from -6 to 6
- quad_weights: float32 [32, 4], P('energy', 'kpt'), may hold values from 0.044194173 to 0.17677669
- orbital_cells: int32 [64, 3072], replicated, may hold values from 0 to 131071
- fixed_charge: float32 [512, 64, 256], P('energy', 'kpt'), may hold values from -16 to 16
- gate_mask: int32 [512, 64, 256], P('energy', 'kpt'), may hold values 0 or 1
- gate_voltage: float32 [512], P('energy'), may hold values from -1 to 1
Outputs:
- potential: float32 [512, 64, 256], P('energy', 'kpt')
- band_shift: float32 [32, 4, 64], P('energy', 'kpt')
Inputs may be any that keep to these rules, and one draw needn't show every extreme that they name: `orbital_cells`: each entry is s * 64 * 256 + y * 256 + z, a cell of one of the layer's 8 planes.
All inputs are finite; a program needn't handle non-finite values. No bound on the sum of `gate_mask` on one device may be relied on, other than what follows from the above.
Results may differ from a plain program's by a relative error of at most 0.0003.
Values sent between devices are 32-bit elements; how exact they have to be, the bound alone decides.
A program may use at most 64 MiB of HBM per device.

v0:
```python
import jax
import jax.numpy as jnp
from jax import lax
from jax.sharding import PartitionSpec as P

LAYER_DEV = 8
SUB = 8
ITERS = 2
PENALTY = 4.0


def with_halo(block, sides, width):
    for axis, dim in sides:
        count = lax.axis_size(axis)
        forward = [(i, i + 1) for i in range(count - 1)]
        backward = [(target, source) for source, target in forward]
        low = lax.ppermute(
            lax.slice_in_dim(block, block.shape[dim] - width, None, axis=dim), axis, forward
        )
        high = lax.ppermute(lax.slice_in_dim(block, 0, width, axis=dim), axis, backward)
        block = jnp.concatenate([low, block, high], axis=dim)
    return block


def operate(values_field, diagonal):
    padded = with_halo(values_field, (("energy", 0), ("kpt", 1)), 1)
    padded = jnp.pad(padded, ((0, 0), (0, 0), (1, 1)))
    beside = padded[2:, 1:-1, 1:-1] + padded[:-2, 1:-1, 1:-1]
    beside = beside + padded[1:-1, 2:, 1:-1] + padded[1:-1, :-2, 1:-1]
    beside = beside + padded[1:-1, 1:-1, 2:] + padded[1:-1, 1:-1, :-2]
    return diagonal * values_field - beside


def paired_sums(residual, image):
    return lax.psum((jnp.sum(residual * residual), jnp.sum(residual * image)), ("energy", "kpt"))


def window_index(map_rows, kpt_index, planes, cross_y, width_y, depth_z):
    section = cross_y * depth_z
    within = map_rows % section
    column = within // depth_z - kpt_index * width_y
    inside = (column >= 0) & (column < width_y)
    layer_rows = lax.broadcasted_iota(jnp.int32, map_rows.shape, 0)
    flat_cell = (
        (layer_rows * planes + map_rows // section) * width_y + jnp.clip(column, 0, width_y - 1)
    ) * depth_z + within % depth_z
    return (flat_cell, inside)


def per_device(density, quad_weights, orbital_cells, fixed_charge, gate_mask, gate_voltage):
    planes_dev, width_y, depth_z = fixed_charge.shape
    kpt_index = lax.axis_index("kpt")
    cross_y = width_y * lax.axis_size("kpt")
    occupancy = jnp.einsum(
        "ek,eklo->lo", quad_weights, density.astype(jnp.float32), precision=lax.Precision.HIGHEST
    )
    partial_rows = lax.psum_scatter(occupancy, "energy", scatter_dimension=0, tiled=True)
    slab_occupancy = lax.psum(partial_rows, "kpt")
    slab_cells = lax.dynamic_slice_in_dim(
        orbital_cells, lax.axis_index("energy") * LAYER_DEV, LAYER_DEV, 0
    )
    flat_cell, inside = window_index(slab_cells, kpt_index, SUB, cross_y, width_y, depth_z)
    deposit = jax.ops.segment_sum(
        jnp.where(inside, slab_occupancy, 0.0).reshape(-1),
        flat_cell.reshape(-1),
        num_segments=planes_dev * width_y * depth_z,
    )
    charge = deposit.reshape(planes_dev, width_y, depth_z)
    gated = gate_mask.astype(jnp.float32)
    diagonal = 6.0 + PENALTY * gated
    right_side = fixed_charge - charge + PENALTY * gated * gate_voltage[:, None, None]
    potential = jnp.zeros_like(right_side)
    residual = right_side
    image = operate(residual, diagonal)
    norm_now, product = paired_sums(residual, image)
    alpha = norm_now / product
    direction = residual
    along = image
    for sweep_index in range(ITERS):
        potential = potential + alpha * direction
        residual = residual - alpha * along
        if sweep_index + 1 < ITERS:
            image = operate(residual, diagonal)
            norm_next, product = paired_sums(residual, image)
            ratio = norm_next / norm_now
            alpha = norm_next / (product - ratio * norm_next / alpha)
            direction = residual + ratio * direction
            along = image + ratio * along
            norm_now = norm_next
    local_values = jnp.where(inside, jnp.take(potential.reshape(-1), flat_cell), 0.0)
    orbital_potential = lax.psum(local_values, "kpt")
    factor = density.shape[3] ** (-0.5)
    block = density.astype(jnp.float32)
    band_shift = (
        jnp.einsum(
            "eklo,lo->ekl",
            block,
            lax.all_gather(orbital_potential, "energy", axis=0, tiled=True),
            precision=lax.Precision.HIGHEST,
        )
        * factor
    )
    return (potential, band_shift)


def solution(mesh):
    in_specs = (
        P("energy", "kpt", None, None),
        P("energy", "kpt"),
        P(),
        P("energy", "kpt", None),
        P("energy", "kpt", None),
        P("energy"),
    )
    out_specs = (P("energy", "kpt", None), P("energy", "kpt", None))
    return jax.shard_map(
        per_device, mesh=mesh, in_specs=in_specs, out_specs=out_specs, check_vma=False
    )
```

profile of v0, /device:TPU:0, one launch (start us, length us, event | category | flops | bytes accessed | tf_op | source)
XLA Modules:
  0.0 549.4 jit_solution(11437265235670384205)
XLA Ops:
  7.2 0.0 copy-start
  7.2 0.0 reduce-scatter.2.cloned.1.call-start
  7.2 1.4 copy-done
  8.6 3.8 fusion.3
  12.4 1.0 copy.38
  13.4 0.0 reduce-scatter.2.cloned.1.call-update
  13.4 0.0 all-reduce.7.cloned.1.call-start
  13.5 1.1 fusion.26
  14.6 36.6 %reduce-scatter.2.cloned.1.call-done = f32[8,3072]{1,0:T(8,128)} async-done(((f32[64,3072]{1,0:T(8,128)}), f32[8,3072]{1,0:T(8,128)}) %reduce-scatter.2.cloned.1.call-update) | async-done | bytes 98320 | tf_op jit(solution)/shard_map/reduce_scatter | solution.py:57
  51.2 0.0 all-reduce.7.cloned.1.call-update
  51.2 0.0 all-reduce.9.cloned.1.call-start
  51.3 0.0 copy-done.5
  51.3 36.7 %all-reduce.7.cloned.1.call-done = f32[8,3072]{1,0:T(8,128)} async-done(((f32[8,3072]{1,0:T(8,128)}), f32[8,3072]{1,0:T(8,128)}) %all-reduce.7.cloned.1.call-update) | async-done | bytes 98320 | tf_op jit(solution)/shard_map/psum | solution.py:58
  88.0 1.1 select_bitcast_fusion
  89.1 128.7 %scatter_custom_fusion = f32[262144]{0:T(1024)S(1)} fusion(s32[24576]{0:T(1024)S(1)} %bitcast.33, f32[24576]{0:T(1024)S(1)} %bitcast.34, f32[]{:T(128)} %constant.72.clone.1), kind=kCustom, calls=%fused_computation.56 | custom fusion | flops 24576 | bytes 1048580 | tf_op jit(solution)/shard_map/scatter-add | solution.py:63
  217.8 1.3 reshape.32
  219.1 2.1 multiply_add_fusion.2
  221.2 1.3 collective-permute-start.1
  222.5 0.0 copy-start.2
  222.5 1.4 collective-permute-start
  223.9 0.0 collective-permute-done.1
  223.9 3.5 collective-permute-done
  227.4 0.1 pad_maximum_fusion.19
  227.5 1.3 collective-permute-start.2
  228.8 4.5 collective-permute-start.3
  233.4 0.4 collective-permute-done.2
  233.8 0.1 copy.12
  233.9 1.5 collective-permute-done.3
  235.4 0.1 copy.14
  235.4 1.2 select_maximum_fusion.4
  236.7 0.0 copy-done.2
  236.7 2.6 multiply_reduce_fusion.1
  239.3 42.2 %all-reduce.3 = (f32[]{:T(128)}, f32[]{:T(128)}) all-reduce(f32[]{:T(128)} %get-tuple-element.7, f32[]{:T(128)} %get-tuple-element.6), channel_id=1, replica_groups=mesh['energy'=8,'kpt'=4] {'energy','kpt'}, use_global_device_ids=true, to_apply=%region_4.5 | all-reduce | flops 2 | bytes 16 | tf_op jit(solution)/shard_map/psum | solution.py:35
  282.8 1.5 multiply_subtract_fusion
  284.3 0.0 copy-start.1
  284.3 1.3 collective-permute-start.5
  285.6 1.3 collective-permute-start.4
  286.9 0.0 collective-permute-done.5
  286.9 4.2 collective-permute-done.4
  291.2 0.1 pad_maximum_fusion.16
  291.3 0.0 copy-start.3
  291.3 1.4 collective-permute-start.6
  292.8 4.5 collective-permute-start.7
  297.3 0.4 collective-permute-done.6
  297.7 0.1 copy.18
  297.8 1.5 collective-permute-done.7
  299.3 0.1 copy.20
  299.3 1.3 select_maximum_fusion
  300.6 0.0 copy-done.1
  300.6 0.0 copy-done.3
  300.6 1.7 fusion.7
  302.3 42.7 %all-reduce.2 = (f32[]{:T(128)}, f32[]{:T(128)}) all-reduce(f32[]{:T(128)} %get-tuple-element.5, f32[]{:T(128)} %get-tuple-element.4), channel_id=1, replica_groups=mesh['energy'=8,'kpt'=4] {'energy','kpt'}, use_global_device_ids=true, to_apply=%region_8.9 | all-reduce | flops 2 | bytes 16 | tf_op jit(solution)/shard_map/psum | solution.py:35
  349.4 1.5 multiply_add_fusion
  350.9 0.0 copy-start.4
  350.9 1.0 copy-done.4
  351.8 0.5 copy.29
  352.4 135.5 %gather_fusion = f32[24576]{0:T(1024)S(1)} fusion(f32[262144]{0:T(1024)S(1)} %bitcast.27, s32[24576]{0:T(1024)S(1)} %broadcast_clamp_fusion), kind=kCustom, calls=%fused_computation | custom fusion | bytes 294912 | tf_op jit(solution)/shard_map/jit(_take)/gather | solution.py:90
  488.0 0.7 select_select_fusion
  488.6 0.0 all-reduce.9.cloned.1.call-update
  488.7 35.5 %all-reduce.9.cloned.1.call-done = f32[8,3072]{1,0:T(8,128)} async-done(((f32[8,3072]{1,0:T(8,128)}), f32[8,3072]{1,0:T(8,128)}) %all-reduce.9.cloned.1.call-update) | async-done | bytes 98320 | tf_op jit(solution)/shard_map/psum | solution.py:91
  524.2 10.7 %all_gather.3 = f32[64,3072]{1,0:T(8,128)S(1)} all-gather(f32[8,3072]{1,0:T(8,128)} %all-reduce.9.cloned.1.call-done), channel_id=1, replica_groups=mesh['energy'=8,'kpt'=4] {'energy'}, dimensions={0}, use_global_device_ids=true | all-gather | bytes 884736 | tf_op jit(solution)/shard_map/all_gather | solution.py:98
  534.8 7.3 %fusion.1 = f32[64,1,4]{2,1,0:T(1,128)S(1)} fusion(bf16[4,64,3072]{2,1,0:T(8,128)(2,1)S(1)} %bitcast.26, f32[64,3072,1]{1,0,2:T(8,128)S(1)} %bitcast.31), kind=kOutput, calls=%fused_computation.13 | convolution fusion | flops 9437184 | bytes 2360320 | tf_op jit(solution)/shard_map/eklo,lo->ekl/dot_general | solution.py:95
  542.2 0.1 copy.26
  542.3 0.6 bitcast_multiply_fusion
  (14 shorter events, 0.1 us)
Async XLA Ops:
  7.2 1.4 copy-start
  7.2 44.0 %reduce-scatter.2.cloned.1.call-start = ((), (), s32[]{:S(2)}) async-start(), calls=%async_computation.1 | async-start | bytes 884736 | tf_op jit(solution)/shard_map/reduce_scatter | solution.py:57
  8.6 42.7 %copy-start.5 = (f32[64]{0:T(128)S(1)}, f32[64]{0:T(128)}, u32[]{:S(2)}) copy-start(f32[64]{0:T(128)} %param.11) | copy-start | bytes 772
  13.4 74.6 %all-reduce.7.cloned.1.call-start = ((), (), s32[]{:S(2)}) async-start(), calls=%async_computation.2 | async-start | bytes 196608 | tf_op jit(solution)/shard_map/psum | solution.py:58
  51.2 472.9 %all-reduce.9.cloned.1.call-start = ((), (), s32[]{:S(2)}) async-start(), calls=%async_computation.3 | async-start | bytes 196608 | tf_op jit(solution)/shard_map/psum | solution.py:91
  221.2 2.7 collective-permute-start.1
  222.5 14.2 %copy-start.2 = (s32[64,16,256]{2,1,0:T(8,128)S(1)}, s32[64,16,256]{2,1,0:T(8,128)}, u32[]{:S(2)}) copy-start(s32[64,16,256]{2,1,0:T(8,128)} %param.10) | copy-start | bytes 3145732
  222.5 4.9 collective-permute-start
  227.5 6.2 %collective-permute-start.2 = (f32[66,1,256]{2,0,1:T(8,128)S(1)}, f32[66,1,256]{2,0,1:T(8,128)S(1)}, u32[]{:S(2)}, u32[]{:S(2)}) collective-permute-start(f32[66,1,256]{2,0,1:T(8,128)S(1)} %copy.11), channel_id=1, source_target_pairs={{1,0},{2,1},{3,2},{5,4},{6,5},{7,6},{9,8},{10,9},{11,10},{13,12},{... | collective-permute-start | bytes 202760 | tf_op jit(solution)/shard_map/ppermute | solution.py:20
  228.8 6.5 %collective-permute-start.3 = (f32[66,1,256]{2,0,1:T(8,128)S(1)}, f32[66,1,256]{2,0,1:T(8,128)S(1)}, u32[]{:S(2)}, u32[]{:S(2)}) collective-permute-start(f32[66,1,256]{2,0,1:T(8,128)S(1)} %copy.13), channel_id=1, source_target_pairs={{0,1},{1,2},{2,3},{4,5},{5,6},{6,7},{8,9},{9,10},{10,11},{12,13},{... | collective-permute-start | bytes 202760 | tf_op jit(solution)/shard_map/ppermute | solution.py:17
  284.3 16.3 %copy-start.1 = (f32[64,16,256]{2,1,0:T(8,128)}, f32[64,16,256]{2,1,0:T(8,128)S(1)}, u32[]{:S(2)}) copy-start(f32[64,16,256]{2,1,0:T(8,128)S(1)} %multiply_subtract_fusion) | copy-start | bytes 3145732
  284.3 2.6 collective-permute-start.5
  285.6 5.6 %collective-permute-start.4 = (f32[1,16,256]{2,1,0:T(8,128)S(1)}, f32[1,16,256]{2,1,0:T(8,128)S(1)}, u32[]{:S(2)}, u32[]{:S(2)}) collective-permute-start(f32[1,16,256]{2,1,0:T(8,128)S(1)} %get-tuple-element.23), channel_id=1, source_target_pairs={{4,0},{8,4},{12,8},{16,12},{20,16},{24,20},{28,24},{5,1},{9,5},{13... | collective-permute-start | bytes 49160 | tf_op jit(solution)/shard_map/ppermute | solution.py:20
  291.3 9.3 %copy-start.3 = (s32[64,16,256]{2,1,0:T(8,128)S(1)}, s32[64,16,256]{2,1,0:T(8,128)}, u32[]{:S(2)}) copy-start(s32[64,16,256]{2,1,0:T(8,128)} %param.10) | copy-start | bytes 3145732
  291.3 6.4 %collective-permute-start.6 = (f32[66,1,256]{2,0,1:T(8,128)S(1)}, f32[66,1,256]{2,0,1:T(8,128)S(1)}, u32[]{:S(2)}, u32[]{:S(2)}) collective-permute-start(f32[66,1,256]{2,0,1:T(8,128)S(1)} %copy.17), channel_id=1, source_target_pairs={{1,0},{2,1},{3,2},{5,4},{6,5},{7,6},{9,8},{10,9},{11,10},{13,12},{... | collective-permute-start | bytes 202760 | tf_op jit(solution)/shard_map/ppermute | solution.py:20
  292.8 6.5 %collective-permute-start.7 = (f32[66,1,256]{2,0,1:T(8,128)S(1)}, f32[66,1,256]{2,0,1:T(8,128)S(1)}, u32[]{:S(2)}, u32[]{:S(2)}) collective-permute-start(f32[66,1,256]{2,0,1:T(8,128)S(1)} %copy.19), channel_id=1, source_target_pairs={{0,1},{1,2},{2,3},{4,5},{5,6},{6,7},{8,9},{9,10},{10,11},{12,13},{... | collective-permute-start | bytes 202760 | tf_op jit(solution)/shard_map/ppermute | solution.py:17
  350.9 1.0 copy-start.4
Sparse Core Ops, SparseCore 0:
  13.5 37.6 reduce-scatter.1
  53.5 34.4 all-reduce.6
  488.8 35.3 all-reduce.8
where the time goes:
time: 550 us; the launch traced here: 549 us
  other arithmetic  144 us (26%)
  local copies, waits for them, and re-layouts  141 us (26%)
  waiting for transfers between devices  120 us (22%)
  blocking collectives  95.6 us (17%)
  between operations  19.7 us (4%)
  starting transfers between devices  17.2 us (3%)
  matrix products  11.1 us (2%)
    gather x2, local copies, waits for them, and re-layouts, per_device(): jnp.take(potential.reshape(-1), flat_cell)  136 us
    scatter-add x1, other arithmetic, per_device(): jax.ops.segment_sum(jnp.where(inside, slab_occupancy, 0.0).reshape(-1), f...  129 us
    psum x2, blocking collectives, paired_sums(): lax.psum((jnp.sum(residual * residual), jnp.sum(residual * image)), ('ene...  84.9 us
    psum x1, waiting for transfers between devices, per_device(): slab_occupancy = lax.psum(partial_rows, 'kpt')  36.7 us
    reduce_scatter x1, waiting for transfers between devices, per_device(): lax.psum_scatter(occupancy, 'energy', scatter_dimension=0, tiled=True)  36.6 us
    psum x1, waiting for transfers between devices, per_device(): orbital_potential = lax.psum(local_values, 'kpt')  35.5 us
    ppermute x4, starting transfers between devices, with_halo(): lax.ppermute(lax.slice_in_dim(block, block.shape[dim] - width, None, axis...  11.7 us
  transfers between devices with their start and end apart: 11, of which 9 were waited for; matrix products, arithmetic and copies ran while one was open for 0% of the time, Pallas kernels for 0%

commit v1 on v0

--- a/solution.py
+++ b/solution.py
@@ -32,7 +32,9 @@
 
 
 def paired_sums(residual, image):
-    return lax.psum((jnp.sum(residual * residual), jnp.sum(residual * image)), ("energy", "kpt"))
+    return lax.psum(
+        lax.psum((jnp.sum(residual * residual), jnp.sum(residual * image)), "kpt"), "energy"
+    )
 
 
 def window_index(map_rows, kpt_index, planes, cross_y, width_y, depth_z):

time: 550 us -> 514 us (0.935)
  blocking collectives: 95.6 us -> 61.1 us
    psum x2 -> x4, blocking collectives: 84.9 us -> 50.4 us  [the longest x2 26.2 us: paired_sums(): lax.psum(lax.psum((jnp.sum(residual * residual), jnp.sum(residual * image...]
where the time goes in v1:
time: 514 us
  other arithmetic  144 us (28%)
  local copies, waits for them, and re-layouts  141 us (27%)
  waiting for transfers between devices  118 us (23%)
  blocking collectives  61.1 us (12%)
  between operations  20.1 us (4%)
  starting transfers between devices  18.2 us (4%)
  matrix products  11.1 us (2%)
    gather x2, local copies, waits for them, and re-layouts, per_device(): jnp.take(potential.reshape(-1), flat_cell)  136 us
    scatter-add x1, other arithmetic, per_device(): jax.ops.segment_sum(jnp.where(inside, slab_occupancy, 0.0).reshape(-1), f...  129 us
    psum x1, waiting for transfers between devices, per_device(): slab_occupancy = lax.psum(partial_rows, 'kpt')  36.7 us
    reduce_scatter x1, waiting for transfers between devices, per_device(): lax.psum_scatter(occupancy, 'energy', scatter_dimension=0, tiled=True)  36.6 us
    psum x1, waiting for transfers between devices, per_device(): orbital_potential = lax.psum(local_values, 'kpt')  35.1 us
    psum x2, blocking collectives, paired_sums(): lax.psum(lax.psum((jnp.sum(residual * residual), jnp.sum(residual * image...  26.2 us
    psum x2, blocking collectives, paired_sums(): lax.psum((jnp.sum(residual * residual), jnp.sum(residual * image)), 'kpt')  24.3 us
    ppermute x4, starting transfers between devices, with_halo(): lax.ppermute(lax.slice_in_dim(block, block.shape[dim] - width, None, axis...  12.6 us
  transfers between devices with their start and end apart: 11, of which 9 were waited for; matrix products, arithmetic and copies ran while one was open for 0% of the time, Pallas kernels for 0%

profile of v1, /device:TPU:0, one launch (start us, length us, event | category | flops | bytes accessed | tf_op | source)
XLA Modules:
  0.0 513.6 jit_solution(14476842822949526027)
XLA Ops:
  7.2 0.0 copy-start
  7.2 0.0 reduce-scatter.2.cloned.1.call-start
  7.2 1.4 copy-done
  8.6 3.8 fusion.3
  12.4 1.0 copy.38
  13.4 0.0 reduce-scatter.2.cloned.1.call-update
  13.4 0.0 all-reduce.9.cloned.1.call-start
  13.5 1.1 fusion.26
  14.6 36.6 %reduce-scatter.2.cloned.1.call-done = f32[8,3072]{1,0:T(8,128)} async-done(((f32[64,3072]{1,0:T(8,128)}), f32[8,3072]{1,0:T(8,128)}) %reduce-scatter.2.cloned.1.call-update) | async-done | bytes 98320 | tf_op jit(solution)/shard_map/reduce_scatter | solution.py:59
  51.2 0.0 all-reduce.9.cloned.1.call-update
  51.2 0.0 all-reduce.11.cloned.1.call-start
  51.3 36.7 %all-reduce.9.cloned.1.call-done = f32[8,3072]{1,0:T(8,128)} async-done(((f32[8,3072]{1,0:T(8,128)}), f32[8,3072]{1,0:T(8,128)}) %all-reduce.9.cloned.1.call-update) | async-done | bytes 98320 | tf_op jit(solution)/shard_map/psum | solution.py:60
  88.0 1.1 select_bitcast_fusion
  89.1 128.7 %scatter_custom_fusion = f32[262144]{0:T(1024)S(1)} fusion(s32[24576]{0:T(1024)S(1)} %bitcast.33, f32[24576]{0:T(1024)S(1)} %bitcast.34, f32[]{:T(128)} %constant.72.clone.1), kind=kCustom, calls=%fused_computation.56 | custom fusion | flops 24576 | bytes 1048580 | tf_op jit(solution)/shard_map/scatter-add | solution.py:65
  217.8 1.3 reshape.32
  219.1 2.1 multiply_add_fusion.2
  221.2 1.3 collective-permute-start.1
  222.5 0.0 copy-start.2
  222.5 1.4 collective-permute-start
  223.9 0.0 collective-permute-done.1
  223.9 3.5 collective-permute-done
  227.4 0.1 pad_maximum_fusion.19
  227.5 1.3 collective-permute-start.2
  228.8 4.5 collective-permute-start.3
  233.4 0.4 collective-permute-done.2
  233.8 0.1 copy.12
  233.9 1.5 collective-permute-done.3
  235.4 0.1 copy.14
  235.4 1.2 select_maximum_fusion.4
  236.7 2.7 multiply_reduce_fusion.1
  239.4 12.9 %all-reduce.5 = (f32[]{:T(128)}, f32[]{:T(128)}) all-reduce(f32[]{:T(128)} %get-tuple-element.7, f32[]{:T(128)} %get-tuple-element.6), channel_id=1, replica_groups=mesh['energy'=8,'kpt'=4] {'kpt'}, use_global_device_ids=true, to_apply=%region_4.5 | all-reduce | flops 2 | bytes 16 | tf_op jit(solution)/shard_map/psum | solution.py:36
  252.3 12.8 %all-reduce.3 = (f32[]{:T(128)}, f32[]{:T(128)}) all-reduce(f32[]{:T(128)} %get-tuple-element.14, f32[]{:T(128)} %get-tuple-element.15), channel_id=1, replica_groups=mesh['energy'=8,'kpt'=4] {'energy'}, use_global_device_ids=true, to_apply=%region_5.6 | all-reduce | flops 2 | bytes 16 | tf_op jit(solution)/shard_map/psum | solution.py:35
  266.4 1.5 multiply_subtract_fusion
  267.9 0.0 copy-start.1
  267.9 2.2 collective-permute-start.5
  270.2 1.3 collective-permute-start.4
  271.5 0.0 collective-permute-done.5
  271.5 2.0 collective-permute-done.4
  273.5 0.1 pad_maximum_fusion.16
  273.6 0.0 copy-start.3
  273.7 1.4 collective-permute-start.6
  275.1 4.5 collective-permute-start.7
  279.7 0.4 collective-permute-done.6
  280.1 0.1 copy.18
  280.1 1.5 collective-permute-done.7
  281.6 0.1 copy.20
  281.7 1.3 select_maximum_fusion
  283.0 0.0 copy-done.1
  283.0 0.0 copy-done.3
  283.0 1.7 fusion.7
  284.6 11.4 %all-reduce.4 = (f32[]{:T(128)}, f32[]{:T(128)}) all-reduce(f32[]{:T(128)} %get-tuple-element.5, f32[]{:T(128)} %get-tuple-element.4), channel_id=1, replica_groups=mesh['energy'=8,'kpt'=4] {'kpt'}, use_global_device_ids=true, to_apply=%region_10.11 | all-reduce | flops 2 | bytes 16 | tf_op jit(solution)/shard_map/psum | solution.py:36
  296.0 13.4 %all-reduce.2 = (f32[]{:T(128)}, f32[]{:T(128)}) all-reduce(f32[]{:T(128)} %get-tuple-element.12, f32[]{:T(128)} %get-tuple-element.13), channel_id=1, replica_groups=mesh['energy'=8,'kpt'=4] {'energy'}, use_global_device_ids=true, to_apply=%region_11.12 | all-reduce | flops 2 | bytes 16 | tf_op jit(solution)/shard_map/psum | solution.py:35
  314.0 1.5 multiply_add_fusion
  315.5 0.0 copy-start.4
  315.5 1.0 copy-done.4
  316.5 0.5 copy.29
  317.0 135.5 %gather_fusion = f32[24576]{0:T(1024)S(1)} fusion(f32[262144]{0:T(1024)S(1)} %bitcast.27, s32[24576]{0:T(1024)S(1)} %broadcast_clamp_fusion), kind=kCustom, calls=%fused_computation | custom fusion | bytes 294912 | tf_op jit(solution)/shard_map/jit(_take)/gather | solution.py:92
  452.6 0.7 select_select_fusion
  453.3 0.0 all-reduce.11.cloned.1.call-update
  453.3 35.1 %all-reduce.11.cloned.1.call-done = f32[8,3072]{1,0:T(8,128)} async-done(((f32[8,3072]{1,0:T(8,128)}), f32[8,3072]{1,0:T(8,128)}) %all-reduce.11.cloned.1.call-update) | async-done | bytes 98320 | tf_op jit(solution)/shard_map/psum | solution.py:93
  488.4 10.7 %all_gather.3 = f32[64,3072]{1,0:T(8,128)S(1)} all-gather(f32[8,3072]{1,0:T(8,128)} %all-reduce.11.cloned.1.call-done), channel_id=1, replica_groups=mesh['energy'=8,'kpt'=4] {'energy'}, dimensions={0}, use_global_device_ids=true | all-gather | bytes 884736 | tf_op jit(solution)/shard_map/all_gather | solution.py:100
  499.1 7.3 %fusion.1 = f32[64,1,4]{2,1,0:T(1,128)S(1)} fusion(bf16[4,64,3072]{2,1,0:T(8,128)(2,1)S(1)} %bitcast.26, f32[64,3072,1]{1,0,2:T(8,128)S(1)} %bitcast.31), kind=kOutput, calls=%fused_computation.13 | convolution fusion | flops 9437184 | bytes 2360320 | tf_op jit(solution)/shard_map/eklo,lo->ekl/dot_general | solution.py:97
  506.4 0.1 copy.26
  506.5 0.6 bitcast_multiply_fusion
  (16 shorter events, 0.2 us)
Async XLA Ops:
  7.2 1.4 copy-start
  7.2 44.0 %reduce-scatter.2.cloned.1.call-start = ((), (), s32[]{:S(2)}) async-start(), calls=%async_computation.1 | async-start | bytes 884736 | tf_op jit(solution)/shard_map/reduce_scatter | solution.py:59
  8.6 42.7 %copy-start.5 = (f32[64]{0:T(128)S(1)}, f32[64]{0:T(128)}, u32[]{:S(2)}) copy-start(f32[64]{0:T(128)} %param.11) | copy-start | bytes 772
  13.4 74.6 %all-reduce.9.cloned.1.call-start = ((), (), s32[]{:S(2)}) async-start(), calls=%async_computation.2 | async-start | bytes 196608 | tf_op jit(solution)/shard_map/psum | solution.py:60
  51.2 437.1 %all-reduce.11.cloned.1.call-start = ((), (), s32[]{:S(2)}) async-start(), calls=%async_computation.3 | async-start | bytes 196608 | tf_op jit(solution)/shard_map/psum | solution.py:93
  221.2 2.7 collective-permute-start.1
  222.5 14.2 %copy-start.2 = (s32[64,16,256]{2,1,0:T(8,128)S(1)}, s32[64,16,256]{2,1,0:T(8,128)}, u32[]{:S(2)}) copy-start(s32[64,16,256]{2,1,0:T(8,128)} %param.10) | copy-start | bytes 3145732
  222.5 4.9 collective-permute-start
  227.5 6.2 %collective-permute-start.2 = (f32[66,1,256]{2,0,1:T(8,128)S(1)}, f32[66,1,256]{2,0,1:T(8,128)S(1)}, u32[]{:S(2)}, u32[]{:S(2)}) collective-permute-start(f32[66,1,256]{2,0,1:T(8,128)S(1)} %copy.11), channel_id=1, source_target_pairs={{1,0},{2,1},{3,2},{5,4},{6,5},{7,6},{9,8},{10,9},{11,10},{13,12},{... | collective-permute-start | bytes 202760 | tf_op jit(solution)/shard_map/ppermute | solution.py:20
  228.8 6.5 %collective-permute-start.3 = (f32[66,1,256]{2,0,1:T(8,128)S(1)}, f32[66,1,256]{2,0,1:T(8,128)S(1)}, u32[]{:S(2)}, u32[]{:S(2)}) collective-permute-start(f32[66,1,256]{2,0,1:T(8,128)S(1)} %copy.13), channel_id=1, source_target_pairs={{0,1},{1,2},{2,3},{4,5},{5,6},{6,7},{8,9},{9,10},{10,11},{12,13},{... | collective-permute-start | bytes 202760 | tf_op jit(solution)/shard_map/ppermute | solution.py:17
  267.9 15.1 %copy-start.1 = (f32[64,16,256]{2,1,0:T(8,128)}, f32[64,16,256]{2,1,0:T(8,128)S(1)}, u32[]{:S(2)}) copy-start(f32[64,16,256]{2,1,0:T(8,128)S(1)} %multiply_subtract_fusion) | copy-start | bytes 3145732
  267.9 3.6 collective-permute-start.5
  270.2 3.4 collective-permute-start.4
  273.6 9.3 %copy-start.3 = (s32[64,16,256]{2,1,0:T(8,128)S(1)}, s32[64,16,256]{2,1,0:T(8,128)}, u32[]{:S(2)}) copy-start(s32[64,16,256]{2,1,0:T(8,128)} %param.10) | copy-start | bytes 3145732
  273.7 6.4 %collective-permute-start.6 = (f32[66,1,256]{2,0,1:T(8,128)S(1)}, f32[66,1,256]{2,0,1:T(8,128)S(1)}, u32[]{:S(2)}, u32[]{:S(2)}) collective-permute-start(f32[66,1,256]{2,0,1:T(8,128)S(1)} %copy.17), channel_id=1, source_target_pairs={{1,0},{2,1},{3,2},{5,4},{6,5},{7,6},{9,8},{10,9},{11,10},{13,12},{... | collective-permute-start | bytes 202760 | tf_op jit(solution)/shard_map/ppermute | solution.py:20
  275.1 6.5 %collective-permute-start.7 = (f32[66,1,256]{2,0,1:T(8,128)S(1)}, f32[66,1,256]{2,0,1:T(8,128)S(1)}, u32[]{:S(2)}, u32[]{:S(2)}) collective-permute-start(f32[66,1,256]{2,0,1:T(8,128)S(1)} %copy.19), channel_id=1, source_target_pairs={{0,1},{1,2},{2,3},{4,5},{5,6},{6,7},{8,9},{9,10},{10,11},{12,13},{... | collective-permute-start | bytes 202760 | tf_op jit(solution)/shard_map/ppermute | solution.py:17
  315.5 1.0 copy-start.4
Sparse Core Ops, SparseCore 0:
  13.5 37.6 reduce-scatter.1
  53.5 34.4 all-reduce.8
  453.4 34.9 all-reduce.10
